TPU v7x, 32 devices: a whole 2x2x4 slice. The times are simulated.
32 devices in a mesh: dp: 8 (over z, x), mlp: 4 (over y, core).
Axes of the slice: x: 2, y: 2, z: 4, core: 2. Of those that a mesh axis runs over, the one named last changes fastest.
Arguments:
- tokens: bfloat16 [32768, 768], P(('dp', 'mlp')), may hold values from -6 to 6
- cotangent: bfloat16 [32768, 768], P(('dp', 'mlp')), may hold values from -6 to 6
- vectors: float32 [14, 768], replicated
- vector_moments: float32 [14, 768], replicated, may hold values from 819.2 to 26214.4
- decays: float32 [2], replicated, may hold values from 0.9 to 0.98
- owner: int32 [4, 3], replicated, may hold values from 0 to 7, as said below
- master_slots: float32 [8, 4, 768, 768], P('dp', 'mlp'), as said below
- left_slots: float32 [8, 4, 768, 768], P('dp', 'mlp'), as said below
- right_slots: float32 [8, 4, 768, 768], P('dp', 'mlp'), as said below
- left_roots: float32 [8, 4, 768, 768], P('dp', 'mlp'), as said below
- right_roots: float32 [8, 4, 768, 768], P('dp', 'mlp'), as said below
- grid_height: int32 [128], P(('dp', 'mlp')), may hold values from 8 to 24, as said below
- grid_width: int32 [128], P(('dp', 'mlp')), may hold values from 8 to 24, as said below
- patch_rows: int32 [32768], P(('dp', 'mlp')), may hold values from 0 to 23, as said below
- patch_cols: int32 [32768], P(('dp', 'mlp')), may hold values from 0 to 23, as said below
- segment: int32 [32768], P(('dp', 'mlp')), may hold values from 0 to 3, as said below
Outputs:
- output: bfloat16 [32768, 768], P(('dp', 'mlp'))
- input_grad: float32 [32768, 768], P(('dp', 'mlp'))
- slot_grads: float32 [8, 4, 768, 768], P('dp', 'mlp')
- new_left: float32 [8, 4, 768, 768], P('dp', 'mlp')
- new_right: float32 [8, 4, 768, 768], P('dp', 'mlp')
- new_master: float32 [8, 4, 768, 768], P('dp', 'mlp')
- vector_grads: float32 [14, 768], P(None, 'mlp')
- new_vector_moments: float32 [14, 768], P(None, 'mlp')
- new_vectors: float32 [14, 768], P(None, 'mlp')
Inputs may be any that keep to these rules, and one draw needn't show every extreme that they name: `owner`: the entries of a row differ; block kind 0 of row m is the m-th of the query, key, value and output projections, kind 1 the m-th 768 columns of the up projection, kind 2 the m-th 768 rows of the down projection. `master_slots`: slot (owner[m,k], m) holds block kind k of row m; the other slots are unused. `left_slots`: symmetric and positive definite. `right_slots`: symmetric and positive definite. `left_roots`: symmetric and positive definite. `right_roots`: symmetric and positive definite. `grid_height`: each image is 16 patches along one side; the other sides of one device's images add up to 64. `grid_width`: as grid_height. `patch_rows`: each device's patches hold its images whole, one after another in the order of their numbers, each in raster order. `patch_cols`: as patch_rows. `segment`: never falls within a device's patches.
All inputs are finite; a program needn't handle non-finite values.
Results may differ from a plain program's by a relative error of at most 0.014.
Values may be sent and summed in bfloat16 or wider, within the bound.
A program may use at most 192 MiB of HBM per device.

v0:
```python
import math
import jax
import jax.numpy as jnp
from jax import lax
from jax.sharding import PartitionSpec as P

HEADS = 12
GRID_BASE = 16
NORM_EPSILON = 1e-06
GRAFT_EPSILON = 1e-06
STEP_EPSILON = 1e-08
RATE_MATRIX = 0.04
RATE_VECTOR = 0.02
MASKED_SCORE = -1e30


def layer_norm(values, gain_row, shift_row):
    centred = values - jnp.mean(values, axis=-1, keepdims=True)
    spread = jnp.mean(centred * centred, axis=-1, keepdims=True)
    return centred * lax.rsqrt(spread + NORM_EPSILON) * gain_row + shift_row


def exact_gelu(values):
    return jax.nn.gelu(values, approximate=False)


def rotate_pairs(flat_values, freq_row, rows_pos, cols_pos):
    tokens_here = flat_values.shape[0]
    values = flat_values.reshape(tokens_here, HEADS, -1)
    half_size = values.shape[-1] // 2
    middle = freq_row.shape[0] // 2
    freq_cols = freq_row[:middle].reshape(HEADS, half_size)
    freq_rows = freq_row[middle:].reshape(HEADS, half_size)
    angle_grid = (
        rows_pos[:, None, None] * freq_rows[None] + cols_pos[:, None, None] * freq_cols[None]
    )
    cosine = jnp.cos(angle_grid)
    sine_part = jnp.sin(angle_grid)
    first_half = values[..., :half_size]
    second = values[..., half_size:]
    turned = jnp.concatenate(
        [first_half * cosine - second * sine_part, second * cosine + first_half * sine_part],
        axis=-1,
    )
    return turned.reshape(tokens_here, -1)


def patch_positions(segment_ids, heights_in, widths_in, rows_in, cols_in):
    images_here = heights_in.shape[0]
    matches = segment_ids[:, None] == jnp.arange(images_here, dtype=jnp.int32)[None, :]
    heights = jnp.sum(jnp.where(matches, heights_in[None, :], 0), axis=1).astype(jnp.float32)
    widths = jnp.sum(jnp.where(matches, widths_in[None, :], 0), axis=1).astype(jnp.float32)
    rows_pos = rows_in.astype(jnp.float32) * GRID_BASE / heights
    cols_pos = cols_in.astype(jnp.float32) * GRID_BASE / widths
    return (rows_pos, cols_pos)


def heads_first(flat_values):
    return jnp.swapaxes(flat_values.reshape(flat_values.shape[0], HEADS, -1), 0, 1)


def tokens_first(stacked):
    return jnp.swapaxes(stacked, 0, 1).reshape(stacked.shape[1], -1)


def local(
    tokens,
    cotangent,
    vectors,
    vector_moments,
    decays,
    owner,
    master_slots,
    left_slots,
    right_slots,
    left_roots,
    right_roots,
    grid_height,
    grid_width,
    patch_rows,
    patch_cols,
    segment,
):
    dp_index = lax.axis_index("dp")
    mlp_index = lax.axis_index("mlp")
    groups_mlp = lax.axis_size("mlp")
    model_width = tokens.shape[1]
    rows_here = tokens.shape[0]
    owner_row = jnp.take(owner, mlp_index, axis=0)
    holds_block = owner_row == dp_index
    owned_blocks = jnp.where(holds_block[:, None, None], master_slots[0, 0][None], 0.0)
    blocks = lax.psum(owned_blocks, "dp")
    blocks_low = blocks.astype(jnp.bfloat16)
    up_rows = vectors[8 : 8 + groups_mlp]
    down_bias = vectors[8 + groups_mlp]
    freq_row = vectors[9 + groups_mlp]
    every_block = lax.all_gather(blocks_low[None], "mlp", axis=0, tiled=True)
    attention_weights = every_block[:, 0]
    up_weight = every_block[:, 1]
    down_weight = every_block[:, 2]
    up_bias = up_rows.reshape(-1)
    inputs = tokens.astype(jnp.float32)
    norm_one, norm_one_back = jax.vjp(layer_norm, inputs, vectors[0], vectors[1])
    norm_one_low = norm_one.astype(jnp.bfloat16)
    query_lin = (
        jnp.dot(norm_one_low, attention_weights[0], preferred_element_type=jnp.float32) + vectors[2]
    )
    key_lin = (
        jnp.dot(norm_one_low, attention_weights[1], preferred_element_type=jnp.float32) + vectors[3]
    )
    value_low = (
        jnp.dot(norm_one_low, attention_weights[2], preferred_element_type=jnp.float32) + vectors[4]
    ).astype(jnp.bfloat16)
    rows_pos, cols_pos = patch_positions(segment, grid_height, grid_width, patch_rows, patch_cols)

    def rotary_map(flat_values, freq_values):
        return rotate_pairs(flat_values, freq_values, rows_pos, cols_pos)

    query_rot, query_back = jax.vjp(rotary_map, query_lin, freq_row)
    key_rot, key_back = jax.vjp(rotary_map, key_lin, freq_row)
    query_heads = heads_first(query_rot.astype(jnp.bfloat16))
    key_heads = heads_first(key_rot.astype(jnp.bfloat16))
    value_heads = heads_first(value_low)
    same_image = segment[:, None] == segment[None, :]
    score_scale = 1.0 / math.sqrt(model_width // HEADS)

    def head_scores(query_head, key_head):
        scores = jnp.dot(query_head, key_head.T, preferred_element_type=jnp.float32) * score_scale
        return jnp.where(same_image, scores, MASKED_SCORE)

    def head_forward(pieces):
        query_head, key_head, value_head = pieces
        scores = head_scores(query_head, key_head)
        row_peak = jnp.max(scores, axis=1, keepdims=True)
        exponent = jnp.exp(scores - row_peak)
        row_total = jnp.sum(exponent, axis=1, keepdims=True)
        weights_low = (exponent / row_total).astype(jnp.bfloat16)
        attended = jnp.dot(weights_low, value_head, preferred_element_type=jnp.float32)
        return (attended, (row_peak + jnp.log(row_total))[:, 0])

    attended_heads, log_totals = lax.map(head_forward, (query_heads, key_heads, value_heads))
    attended_low = tokens_first(attended_heads).astype(jnp.bfloat16)
    branch_one = (
        jnp.dot(attended_low, attention_weights[3], preferred_element_type=jnp.float32) + vectors[5]
    )
    middle = inputs + branch_one
    norm_two, norm_two_back = jax.vjp(layer_norm, middle, vectors[6], vectors[7])
    norm_two_low = norm_two.astype(jnp.bfloat16)
    pre_act = (
        jnp.einsum(
            "td,mde->tme", norm_two_low, up_weight, preferred_element_type=jnp.float32
        ).reshape(rows_here, -1)
        + up_bias
    )
    activation, gelu_back = jax.vjp(exact_gelu, pre_act)
    activation_blocks = activation.astype(jnp.bfloat16).reshape(rows_here, groups_mlp, -1)
    branch_two = (
        jnp.einsum(
            "tme,med->td", activation_blocks, down_weight, preferred_element_type=jnp.float32
        )
        + down_bias
    )
    grad_act = jnp.einsum(
        "td,med->tme", cotangent, down_weight, preferred_element_type=jnp.float32
    ).reshape(rows_here, -1)
    grad_down = jnp.einsum(
        "tme,td->med", activation_blocks, cotangent, preferred_element_type=jnp.float32
    )
    grad_pre_blocks = gelu_back(grad_act)[0].astype(jnp.bfloat16).reshape(rows_here, groups_mlp, -1)
    grad_up = jnp.einsum(
        "td,tme->mde", norm_two_low, grad_pre_blocks, preferred_element_type=jnp.float32
    )
    up_grad_rows = jnp.sum(grad_pre_blocks, axis=0, dtype=jnp.float32)
    grad_norm_two = jnp.einsum(
        "tme,mde->td", grad_pre_blocks, up_weight, preferred_element_type=jnp.float32
    )
    output_low = (middle + branch_two).astype(jnp.bfloat16)
    grad_middle_norm, grad_gain_two, grad_shift_two = norm_two_back(grad_norm_two)
    grad_middle = cotangent.astype(jnp.float32) + grad_middle_norm
    grad_branch_low = grad_middle.astype(jnp.bfloat16)
    grad_out_bias = jnp.sum(grad_branch_low, axis=0, dtype=jnp.float32)
    grad_out_weight = jnp.dot(attended_low.T, grad_branch_low, preferred_element_type=jnp.float32)
    grad_attended_low = jnp.dot(
        grad_branch_low, attention_weights[3].T, preferred_element_type=jnp.float32
    ).astype(jnp.bfloat16)

    def head_backward(pieces):
        query_head, key_head, value_head, grad_head, log_total = pieces
        scores = head_scores(query_head, key_head)
        probs = jnp.exp(scores - log_total[:, None])
        grad_probs = jnp.dot(grad_head, value_head.T, preferred_element_type=jnp.float32)
        inner = jnp.sum(probs * grad_probs, axis=1, keepdims=True)
        grad_scores = (probs * (grad_probs - inner)).astype(jnp.bfloat16)
        grad_query = (
            jnp.dot(grad_scores, key_head, preferred_element_type=jnp.float32) * score_scale
        )
        grad_key = (
            jnp.dot(grad_scores.T, query_head, preferred_element_type=jnp.float32) * score_scale
        )
        grad_value = jnp.dot(
            probs.astype(jnp.bfloat16).T, grad_head, preferred_element_type=jnp.float32
        )
        return (grad_query, grad_key, grad_value)

    grad_queries, grad_keys, grad_values = lax.map(
        head_backward,
        (query_heads, key_heads, value_heads, heads_first(grad_attended_low), log_totals),
    )
    grad_query_lin, grad_freq_query = query_back(tokens_first(grad_queries))
    grad_key_lin, grad_freq_key = key_back(tokens_first(grad_keys))
    grad_query_low = grad_query_lin.astype(jnp.bfloat16)
    grad_key_low = grad_key_lin.astype(jnp.bfloat16)
    grad_value_low = tokens_first(grad_values).astype(jnp.bfloat16)
    grad_query_weight = jnp.dot(norm_one_low.T, grad_query_low, preferred_element_type=jnp.float32)
    grad_key_weight = jnp.dot(norm_one_low.T, grad_key_low, preferred_element_type=jnp.float32)
    grad_value_weight = jnp.dot(norm_one_low.T, grad_value_low, preferred_element_type=jnp.float32)
    grad_norm_one = jnp.dot(
        grad_query_low, attention_weights[0].T, preferred_element_type=jnp.float32
    )
    grad_norm_one = grad_norm_one + jnp.dot(
        grad_key_low, attention_weights[1].T, preferred_element_type=jnp.float32
    )
    grad_norm_one = grad_norm_one + jnp.dot(
        grad_value_low, attention_weights[2].T, preferred_element_type=jnp.float32
    )
    grad_input_norm, grad_gain_one, grad_shift_one = norm_one_back(grad_norm_one)
    input_grad = grad_middle + grad_input_norm
    head_rows = jnp.stack(
        [
            grad_gain_one,
            grad_shift_one,
            jnp.sum(grad_query_low, axis=0, dtype=jnp.float32),
            jnp.sum(grad_key_low, axis=0, dtype=jnp.float32),
            jnp.sum(grad_value_low, axis=0, dtype=jnp.float32),
            grad_out_bias,
            grad_gain_two,
            grad_shift_two,
        ]
    )
    tail_rows = jnp.stack(
        [jnp.sum(cotangent, axis=0, dtype=jnp.float32), grad_freq_query + grad_freq_key]
    )
    local_vectors = jnp.concatenate([head_rows, up_grad_rows, tail_rows], axis=0)
    vector_sum = lax.psum(local_vectors, ("dp", "mlp"))
    attention_grads = jnp.stack(
        [grad_query_weight, grad_key_weight, grad_value_weight, grad_out_weight]
    )
    attention_share, up_share, down_share = (
        lax.psum_scatter(
            attention_grads.astype(jnp.bfloat16), "mlp", scatter_dimension=0, tiled=True
        ).astype(jnp.float32),
        lax.psum_scatter(
            grad_up.astype(jnp.bfloat16), "mlp", scatter_dimension=0, tiled=True
        ).astype(jnp.float32),
        lax.psum_scatter(
            grad_down.astype(jnp.bfloat16), "mlp", scatter_dimension=0, tiled=True
        ).astype(jnp.float32),
    )
    grad_stack = jnp.concatenate([attention_share, up_share, down_share], axis=0)
    reduced = lax.psum(grad_stack, "dp")
    block_kind = jnp.sum(jnp.where(holds_block, jnp.arange(3, dtype=jnp.int32), 0))
    owns_block = jnp.any(holds_block)
    gradient = jnp.take(reduced, block_kind, axis=0)
    decay_matrix = decays[0]
    left_old = left_slots[0, 0]
    right_old = right_slots[0, 0]
    master_old = master_slots[0, 0]
    left_next = decay_matrix * left_old + (1.0 - decay_matrix) * jnp.dot(
        gradient, gradient.T, precision=lax.Precision.HIGHEST
    )
    right_next = decay_matrix * right_old + (1.0 - decay_matrix) * jnp.dot(
        gradient.T, gradient, precision=lax.Precision.HIGHEST
    )
    direction = jnp.dot(
        jnp.dot(left_roots[0, 0], gradient, precision=lax.Precision.HIGHEST),
        right_roots[0, 0],
        precision=lax.Precision.HIGHEST,
    )
    normed_step = direction * lax.rsqrt(jnp.mean(direction * direction) + GRAFT_EPSILON)
    master_next = master_old - RATE_MATRIX * normed_step
    slot_grad = jnp.where(owns_block, gradient, 0.0)[None, None]
    left_out = jnp.where(owns_block, left_next, left_old)[None, None]
    right_out = jnp.where(owns_block, right_next, right_old)[None, None]
    master_out = jnp.where(owns_block, master_next, master_old)[None, None]
    share_width = model_width // groups_mlp

    def own_columns(table):
        return lax.dynamic_slice_in_dim(table, mlp_index * share_width, share_width, 1)

    grad_share = own_columns(vector_sum)
    moment_old = own_columns(vector_moments)
    vector_old = own_columns(vectors)
    decay_vector = decays[1]
    moment_next = decay_vector * moment_old + (1.0 - decay_vector) * grad_share * grad_share
    vector_next = vector_old - RATE_VECTOR * grad_share / (jnp.sqrt(moment_next) + STEP_EPSILON)
    return (
        output_low,
        input_grad,
        slot_grad,
        left_out,
        right_out,
        master_out,
        grad_share,
        moment_next,
        vector_next,
    )


def solution(mesh):
    placed = (
        P(("dp", "mlp"), None),
        P(("dp", "mlp"), None),
        P(),
        P(),
        P(),
        P(),
        P("dp", "mlp", None, None),
        P("dp", "mlp", None, None),
        P("dp", "mlp", None, None),
        P("dp", "mlp", None, None),
        P("dp", "mlp", None, None),
        P(("dp", "mlp")),
        P(("dp", "mlp")),
        P(("dp", "mlp")),
        P(("dp", "mlp")),
        P(("dp", "mlp")),
    )
    return jax.shard_map(
        local,
        mesh=mesh,
        in_specs=placed,
        out_specs=(
            P(("dp", "mlp"), None),
            P(("dp", "mlp"), None),
            P("dp", "mlp", None, None),
            P("dp", "mlp", None, None),
            P("dp", "mlp", None, None),
            P("dp", "mlp", None, None),
            P(None, "mlp"),
            P(None, "mlp"),
            P(None, "mlp"),
        ),
        check_vma=False,
    )
```

profile of v0, /device:TPU:0, one launch (start us, length us, event | category | flops | bytes accessed | tf_op | source)
XLA Modules:
  0.0 1202.3 jit_solution(14143546167382789815)
XLA Ops:
  8.8 5.2 broadcast_select_fusion
  14.0 278.3 %all-reduce.12 = bf16[3,768,768]{2,1,0:T(8,128)(2,1)} all-reduce(f32[3,768,768]{2,1,0:T(8,128)} %broadcast_select_fusion), channel_id=1, replica_groups=mesh['dp'=8,'mlp'=4] {'dp'}, use_global_device_ids=true, to_apply=%region_2.3 | all-reduce | flops 1769472 | bytes 10616832 | tf_op jit(solution)/shard_map/psum | solution.py:92
  294.8 2.6 copy.100
  303.2 78.7 %all-gather.3.cloned.1.call-done = bf16[12,768,768]{2,1,0:T(8,128)(2,1)} async-done(((bf16[3,768,768]{2,1,0:T(8,128)(2,1)}), bf16[12,768,768]{2,1,0:T(8,128)(2,1)}) %all-gather.3.cloned.1.call-update) | async-done | bytes 14155792 | tf_op jit(solution)/shard_map/all_gather | solution.py:97
  381.8 4.9 slice_bitcast_fusion.3
  386.7 2.9 convolution_add_fusion
  389.7 3.8 convolution_add_fusion.1
  393.6 7.7 subtract_convert_fusion
  402.5 4.1 copy.102
  409.1 4.1 copy.103
  413.2 4.5 add_convert_fusion.4
  417.7 4.1 copy.101
  421.8 85.7 %while.32 = (s32[]{:T(128)}, bf16[12,1024,64]{1,2,0:T(8,128)(2,1)}, f32[12,1024]{1,0:T(8,128)}, bf16[12,1024,64]{2,1,0:T(8,128)(2,1)}, bf16[12,1024,64]{2,1,0:T(...) while((s32[]{:T(128)}, bf16[12,1024,64]{1,2,0:T(8,128)(2,1)}, ...), condition=%wide.region_8.9_spmd.clone.clone, body=%wide.region_5.8_spmd.clone.sunk.clone | while | flops 284163072 | bytes 13695065 | solution.py:141
  424.6 3.0 fusion.195
  431.7 3.0 fusion.195
  438.9 3.0 fusion.195
  446.0 3.0 fusion.195
  453.2 3.0 fusion.195
  460.3 3.0 fusion.195
  467.4 3.0 fusion.195
  474.6 3.0 fusion.195
  481.7 3.0 fusion.195
  488.9 3.0 fusion.195
  496.0 3.0 fusion.195
  503.1 3.0 fusion.195
  507.5 10.2 fusion.64
  517.7 12.7 %copy.133 = f32[1024,3072]{1,0:T(8,128)} copy(f32[1024,3072]{0,1:T(8,128)} %bitcast.277) | data formatting | bytes 25165824 | tf_op jit(solution)/shard_map/reshape | solution.py:165
  530.3 6.6 copy.105
  537.0 4.0 fusion.140
  544.0 40.9 %convert_reduce_fusion = (f32[3072]{0:T(1024)}, bf16[1024,3072]{1,0:T(8,128)(2,1)}, f32[1024,3072]{1,0:T(8,128)}, f32[1024,3072]{1,0:T(8,128)}) fusion(f32[1024,3072]{1,0:T(8,128)S(1)} %copy-done.14, f32[3072]{0:T(1024)S(1)} %add.236, bf16[3072,768]{1,0:T(8,128)(2,1)} %bitcast.289, f32[1024,768]{0,1:T(8,128)S(1)} %get-tuple-element.370, ...), kind=kOutput, calls=%fused_computation.58 | convolution fusion | flops 5071696896 | bytes 51943424 | tf_op jit(solution)/shard_map/td,mde->tme/dot_general | solution.py:150
  584.9 12.8 %multiply_convert_fusion.1 = bf16[1024,3072]{1,0:T(8,128)(2,1)} fusion(f32[1024,3072]{1,0:T(8,128)} %get-tuple-element.336, f32[1024,3072]{1,0:T(8,128)} %get-tuple-element.371, f32[3072]{0:T(1024)S(1)} %add.236), kind=kLoop, calls=%fused_computation.60 | loop fusion | flops 12582912 | bytes 31469568 | tf_op jit(solution)/shard_map/convert_element_type | solution.py:156
  597.8 8.6 copy.137
  606.4 9.0 convolution_convert_fusion
  618.0 8.8 copy.138
  626.8 9.9 fusion.141
  636.7 3.5 copy.112
  640.2 3.9 multiply_reduce_fusion.1
  647.4 4.4 convolution_convert_fusion.1
  651.8 4.1 copy.113
  655.9 10.4 convert_bitcast_fusion
  667.0 159.3 %while.33 = (s32[]{:T(128)}, f32[12,1024,64]{1,2,0:T(8,128)}, f32[12,1024,64]{1,2,0:T(8,128)}, bf16[12,1024,64]{1,2,0:T(8,128)(2,1)}, bf16[12,1024,64]{2,1,0:T(8...) while((s32[]{:T(128)}, f32[12,1024,64]{1,2,0:T(8,128)}, ...), condition=%wide.region_15.16_spmd.clone.clone, body=%wide.region_13.15_spmd.clone.sunk.clone | while | flops 681704448 | bytes 34112624 | solution.py:205
  669.7 2.6 multiply_reduce_fusion.11
  683.0 2.6 multiply_reduce_fusion.11
  709.5 2.6 multiply_reduce_fusion.11
  722.8 2.6 multiply_reduce_fusion.11
  736.0 2.6 multiply_reduce_fusion.11
  775.8 2.6 multiply_reduce_fusion.11
  826.3 12.0 multiply_add_fusion.1
  840.7 7.8 multiply_add_fusion
  860.6 48.4 %reduce-scatter.4.cloned.1.call-done = bf16[1,768,768]{2,1,0:T(8,128)(2,1)} async-done(((bf16[4,768,768]{2,1,0:T(8,128)(2,1)}), bf16[1,768,768]{2,1,0:T(8,128)(2,1)}) %reduce-scatter.4.cloned.1.call-update) | async-done | bytes 1179664 | tf_op jit(solution)/shard_map/reduce_scatter | solution.py:249
  909.0 5.3 maximum_convert_fusion
  919.4 10.5 fusion.75
  932.5 3.3 fusion.114
  935.8 2.8 fusion.115
  938.6 3.1 fusion.133
  944.2 3.3 convert_reduce_fusion.2
  947.5 3.6 copy.125
  955.9 45.1 %psum.23 = f32[14,768]{1,0:T(8,128)S(1)} all-reduce(f32[14,768]{1,0:T(8,128)S(1)} %concatenate.21), channel_id=1, replica_groups=mesh['dp'=8,'mlp'=4] {'dp','mlp'}, use_global_device_ids=true, to_apply=%region_39.40 | all-reduce | flops 10752 | bytes 86016 | tf_op jit(solution)/shard_map/psum | solution.py:244
  1003.1 143.9 %all-reduce.11.cloned.1.call-done = f32[3,768,768]{2,1,0:T(8,128)} async-done(((f32[3,768,768]{2,1,0:T(8,128)}), f32[3,768,768]{2,1,0:T(8,128)}) %all-reduce.11.cloned.1.call-update) | async-done | bytes 7077904 | tf_op jit(solution)/shard_map/psum | solution.py:260
  1147.1 13.6 %fusion.79 = f32[768,768]{1,0:T(8,128)S(1)} fusion(f32[1,1,768,768]{3,2,1,0:T(8,128)} %param.29, f32[3,768,768]{2,1,0:T(8,128)} %all-reduce.11.cloned.1.call-done, s32[]{:T(128)S(6)} %select_n.95, pred[]{:T(512)S(6)} %and.13), kind=kOutput, calls=%fused_computation.124 | convolution fusion | flops 5436407808 | bytes 7077893 | tf_op jit(solution)/shard_map/dot_general | solution.py:275
  1160.7 8.7 multiply_reduce_fusion.4
  1170.1 5.0 fusion.76
  1177.5 8.9 fusion.84
  1186.4 9.2 fusion.82
  (315 shorter events, 247.0 us)
Async XLA Ops:
  7.2 1153.5 %copy-start = (f32[1,1,768,768]{3,2,1,0:T(8,128)S(1)}, f32[1,1,768,768]{3,2,1,0:T(8,128)}, u32[]{:S(2)}) copy-start(f32[1,1,768,768]{3,2,1,0:T(8,128)} %param.30) | copy-start | bytes 7077892
  7.2 374.6 %all-gather.3.cloned.1.call-start = ((), (), s32[]{:S(2)}) async-start(), calls=%async_computation.7 | async-start | bytes 17694720 | tf_op jit(solution)/shard_map/all_gather | solution.py:97
  292.3 568.3 %reduce-scatter.8.cloned.1.call-start = ((), (), s32[]{:S(2)}) async-start(), calls=%async_computation.5 | async-start | bytes 5898240 | tf_op jit(solution)/shard_map/reduce_scatter | solution.py:255
  292.5 1.1 copy-start.9
  293.7 3.8 copy-start.38
  293.7 4.0 slice-start
  293.7 4.0 copy-start.20
  293.7 4.0 copy-start.53
  293.7 4.0 copy-start.54
  294.8 8.3 copy-start.50
  294.8 8.3 copy-start.51
  297.5 96.0 %copy-start.28 = (f32[12,32]{1,0:T(8,128)}, f32[12,32]{1,0:T(8,128)S(1)}, u32[]{:S(2)}) copy-start(f32[12,32]{1,0:T(8,128)S(1)} %mul.390) | copy-start | bytes 4612
  297.6 95.9 %copy-start.30 = (f32[12,32]{1,0:T(8,128)}, f32[12,32]{1,0:T(8,128)S(1)}, u32[]{:S(2)}) copy-start(f32[12,32]{1,0:T(8,128)S(1)} %mul.385) | copy-start | bytes 4612
  298.4 114.8 %copy-start.40 = (f32[768]{0:T(1024)}, f32[768]{0:T(1024)S(1)}, u32[]{:S(2)}) copy-start(f32[768]{0:T(1024)S(1)} %get-tuple-element.290) | copy-start | bytes 9220
  298.4 114.8 %copy-start.48 = (f32[768]{0:T(1024)}, f32[768]{0:T(1024)S(1)}, u32[]{:S(2)}) copy-start(f32[768]{0:T(1024)S(1)} %get-tuple-element.289) | copy-start | bytes 9220
  300.4 112.8 %copy-start.32 = (f32[1024]{0:T(1024)}, f32[1024]{0:T(1024)S(1)}, u32[]{:S(2)}) copy-start(f32[1024]{0:T(1024)S(1)} %broadcast_multiply_fusion.1) | copy-start | bytes 12292
  302.5 0.6 copy-start.44
  302.5 110.7 %copy-start.42 = (f32[1024]{0:T(1024)}, f32[1024]{0:T(1024)S(1)}, u32[]{:S(2)}) copy-start(f32[1024]{0:T(1024)S(1)} %fusion.118) | copy-start | bytes 12292
  303.1 90.4 %copy-start.34 = (f32[1024]{0:T(1024)}, f32[1024]{0:T(1024)S(1)}, u32[]{:S(2)}) copy-start(f32[1024]{0:T(1024)S(1)} %get-tuple-element.377) | copy-start | bytes 12292
  303.1 90.4 %copy-start.36 = (f32[1024]{0:T(1024)}, f32[1024]{0:T(1024)S(1)}, u32[]{:S(2)}) copy-start(f32[1024]{0:T(1024)S(1)} %get-tuple-element.378) | copy-start | bytes 12292
  381.8 4.9 copy-start.1
  389.7 3.9 copy-start.15
  393.5 7.8 copy-start.17
  537.0 7.0 copy-start.14
  541.0 43.9 %copy-start.4 = (f32[1024,768]{0,1:T(8,128)}, f32[1024,768]{0,1:T(8,128)S(1)}, u32[]{:S(2)}) copy-start(f32[1024,768]{0,1:T(8,128)S(1)} %get-tuple-element.370) | copy-start | bytes 9437188
  615.4 245.2 %reduce-scatter.6.cloned.1.call-start = ((), (), s32[]{:S(2)}) async-start(), calls=%async_computation.4 | async-start | bytes 5898240 | tf_op jit(solution)/shard_map/reduce_scatter | solution.py:252
  640.2 3.9 copy-start.5
  640.2 4.7 copy-start.8
  644.9 1.4 copy-start.12
  645.7 1.7 copy-start.6
  647.4 4.4 copy-start.23
  666.3 0.7 copy-start.21
  666.3 242.7 %reduce-scatter.4.cloned.1.call-start = ((), (), s32[]{:S(2)}) async-start(), calls=%async_computation.3 | async-start | bytes 5898240 | tf_op jit(solution)/shard_map/reduce_scatter | solution.py:249
  667.0 159.3 %copy-start.29 = (f32[12,32]{1,0:T(8,128)S(1)}, f32[12,32]{1,0:T(8,128)}, u32[]{:S(2)}) copy-start(f32[12,32]{1,0:T(8,128)} %copy-done.28) | copy-start | bytes 4612
  667.0 159.3 %copy-start.31 = (f32[12,32]{1,0:T(8,128)S(1)}, f32[12,32]{1,0:T(8,128)}, u32[]{:S(2)}) copy-start(f32[12,32]{1,0:T(8,128)} %copy-done.30) | copy-start | bytes 4612
  667.0 159.3 %copy-start.35 = (f32[1024]{0:T(1024)S(1)}, f32[1024]{0:T(1024)}, u32[]{:S(2)}) copy-start(f32[1024]{0:T(1024)} %copy-done.34) | copy-start | bytes 12292
  667.0 159.3 %copy-start.37 = (f32[1024]{0:T(1024)S(1)}, f32[1024]{0:T(1024)}, u32[]{:S(2)}) copy-start(f32[1024]{0:T(1024)} %copy-done.36) | copy-start | bytes 12292
  826.3 12.3 %copy-start.18 = (f32[12,1024,64]{1,2,0:T(8,128)S(1)}, f32[12,1024,64]{1,2,0:T(8,128)}, u32[]{:S(2)}) copy-start(f32[12,1024,64]{1,2,0:T(8,128)} %get-tuple-element.104) | copy-start | bytes 9437188
  838.3 2.5 copy-start.16
  838.5 17.7 %copy-start.25 = (bf16[1024,12,64]{0,2,1:T(8,128)(2,1)}, bf16[1024,12,64]{0,2,1:T(8,128)(2,1)S(1)}, u32[]{:S(2)}) copy-start(bf16[1024,12,64]{0,2,1:T(8,128)(2,1)S(1)} %get-tuple-element.342) | copy-start | bytes 4718596
  848.6 1.4 copy-start.22
  848.6 1.9 copy-start.24
  850.5 4.1 copy-start.26
  850.5 2.0 copy-start.2
  850.5 2.4 copy-start.10
  850.5 2.4 copy-start.33
  850.5 2.4 copy-start.41
  850.5 2.4 copy-start.43
  850.5 2.4 copy-start.49
  860.3 286.7 %all-reduce.11.cloned.1.call-start = ((), (), s32[]{:S(2)}) async-start(), calls=%async_computation.6 | async-start | bytes 14155776 | tf_op jit(solution)/shard_map/psum | solution.py:260
  914.4 1.9 copy-start.52
  914.4 5.1 copy-start.47
  932.5 3.3 copy-start.27
  935.7 2.8 copy-start.3
  935.8 2.8 copy-start.11
  938.6 3.2 copy-start.45
  941.7 1.9 copy-start.7
  941.8 2.4 copy-start.13
  947.5 5.5 copy-start.46
  951.0 50.0 %copy-start.39 = (f32[14,768]{1,0:T(8,128)S(1)}, f32[14,768]{1,0:T(8,128)}, u32[]{:S(2)}) copy-start(f32[14,768]{1,0:T(8,128)} %param.22) | copy-start | bytes 129028
  1170.1 5.0 copy-start.19
  1175.1 2.4 copy-start.55
  1177.5 8.9 copy-start.56
Sparse Core Ops, SparseCore 0:
  292.4 89.3 all-gather.2
  615.5 47.9 reduce-scatter.7
  666.4 48.3 reduce-scatter.5
  860.4 48.5 reduce-scatter.3
  914.5 232.5 all-reduce.10
where the time goes:
time: 1220 us; the launch traced here: 1200 us
  matrix products  359 us (29%)
  blocking collectives  323 us (26%)
  waiting for transfers between devices  271 us (22%)
  local copies, waits for them, and re-layouts  115 us (9%)
  other arithmetic  115 us (9%)
  between operations  18.4 us (2%)
    psum x1, blocking collectives, local(): blocks = lax.psum(owned_blocks, 'dp')  278 us
    psum x1, waiting for transfers between devices, local(): reduced = lax.psum(grad_stack, 'dp')  144 us
    all_gather x1, waiting for transfers between devices, local(): every_block = lax.all_gather(blocks_low[None], 'mlp', axis=0, tiled=True)  78.7 us
    dot_general x24, matrix products, head_scores(): jnp.dot(query_head, key_head.T, preferred_element_type=jnp.float32)  52.2 us
    reduce_scatter x1, waiting for transfers between devices, local(): lax.psum_scatter(attention_grads.astype(jnp.bfloat16), 'mlp', scatter_dim...  48.4 us
    psum x1, blocking collectives, local(): vector_sum = lax.psum(local_vectors, ('dp', 'mlp'))  45.1 us
    dot_general x1, matrix products, local(): jnp.einsum('td,mde->tme', norm_two_low, up_weight, preferred_element_type...  40.9 us
    dot_general x12, matrix products, head_forward(): jnp.dot(weights_low, value_head, preferred_element_type=jnp.float32)  35.5 us
  transfers between devices with their start and end apart: 5, of which 3 were waited for; matrix products, arithmetic and copies ran while one was open for 24% of the time, Pallas kernels for 0%

commit v1 on v0

--- a/solution.py
+++ b/solution.py
@@ -1,3 +1,4 @@
+import functools
 import math
 import jax
 import jax.numpy as jnp
@@ -12,6 +13,14 @@
 RATE_MATRIX = 0.04
 RATE_VECTOR = 0.02
 MASKED_SCORE = -1e30
+
+
+def surface_shape(in_array, axis_name):
+    tile_out = lax.all_gather(in_array, axis_name=axis_name)
+    return jnp.sum(tile_out, axis=0)
+
+
+mark_trees = functools.partial(surface_shape, axis_name="dp")
 
 
 def layer_norm(values, gain_row, shift_row):
@@ -257,7 +266,7 @@
         ).astype(jnp.float32),
     )
     grad_stack = jnp.concatenate([attention_share, up_share, down_share], axis=0)
-    reduced = lax.psum(grad_stack, "dp")
+    reduced = mark_trees(grad_stack)
     block_kind = jnp.sum(jnp.where(holds_block, jnp.arange(3, dtype=jnp.int32), 0))
     owns_block = jnp.any(holds_block)
     gradient = jnp.take(reduced, block_kind, axis=0)

time: 1220 us -> 2090 us (1.71)
  waiting for transfers between devices: 271 us -> 1060 us
  blocking collectives: 323 us -> 370 us
  other arithmetic: 115 us -> 138 us
    all_gather x0 -> x1, waiting for transfers between devices: none -> 937 us  [surface_shape(): tile_out = lax.all_gather(in_array, axis_name=axis_name)]
    psum x1 -> x0, waiting for transfers between devices: 144 us -> none  [local(): reduced = lax.psum(grad_stack, 'dp')]
    psum x1, blocking collectives: 45.1 us -> 91.3 us  [local(): vector_sum = lax.psum(local_vectors, ('dp', 'mlp'))]
    reduce_sum x0 -> x1, other arithmetic: none -> 21.5 us  [surface_shape(): return jnp.sum(tile_out, axis=0)]
  transfers between devices with their start and end apart: 5 -> 5, of which waited for: 3 -> 3; matrix products, arithmetic and copies ran while one was open for 24% -> 14% of each run, Pallas kernels for 0% -> 0%
where the time goes in v1:
time: 2090 us; the launch traced here: 2080 us
  waiting for transfers between devices  1060 us (51%)
  matrix products  371 us (18%)
  blocking collectives  370 us (18%)
  other arithmetic  138 us (7%)
  local copies, waits for them, and re-layouts  115 us (6%)
    all_gather x1, waiting for transfers between devices, surface_shape(): tile_out = lax.all_gather(in_array, axis_name=axis_name)  937 us
    psum x1, blocking collectives, local(): blocks = lax.psum(owned_blocks, 'dp')  278 us
    psum x1, blocking collectives, local(): vector_sum = lax.psum(local_vectors, ('dp', 'mlp'))  91.3 us
    all_gather x1, waiting for transfers between devices, local(): every_block = lax.all_gather(blocks_low[None], 'mlp', axis=0, tiled=True)  78.6 us
    dot_general x24, matrix products, head_scores(): jnp.dot(query_head, key_head.T, preferred_element_type=jnp.float32)  52.2 us
    reduce_scatter x1, waiting for transfers between devices, local(): lax.psum_scatter(attention_grads.astype(jnp.bfloat16), 'mlp', scatter_dim...  48.2 us
  transfers between devices with their start and end apart: 5, of which 3 were waited for; matrix products, arithmetic and copies ran while one was open for 14% of the time, Pallas kernels for 0%

profile of v1, /device:TPU:0, one launch (start us, length us, event | category | flops | bytes accessed | tf_op | source)
XLA Modules:
  0.0 2076.7 jit_solution(3306265024773778636)
XLA Ops:
  8.7 5.2 broadcast_select_fusion
  14.0 278.3 %all-reduce.9 = bf16[3,768,768]{2,1,0:T(8,128)(2,1)} all-reduce(f32[3,768,768]{2,1,0:T(8,128)} %broadcast_select_fusion), channel_id=1, replica_groups=mesh['dp'=8,'mlp'=4] {'dp'}, use_global_device_ids=true, to_apply=%region_2.3 | all-reduce | flops 1769472 | bytes 10616832 | tf_op jit(solution)/shard_map/psum | solution.py:101
  294.8 2.6 copy.100
  303.2 78.6 %all-gather.5.cloned.1.call-done = bf16[12,768,768]{2,1,0:T(8,128)(2,1)} async-done(((bf16[3,768,768]{2,1,0:T(8,128)(2,1)}), bf16[12,768,768]{2,1,0:T(8,128)(2,1)}) %all-gather.5.cloned.1.call-update) | async-done | bytes 14155792 | tf_op jit(solution)/shard_map/all_gather | solution.py:106
  381.8 4.9 slice_bitcast_fusion.3
  386.7 2.9 convolution_add_fusion
  389.7 3.8 convolution_add_fusion.1
  393.5 7.7 subtract_convert_fusion
  402.5 4.1 copy.102
  409.1 4.2 copy.103
  413.2 4.5 add_convert_fusion.4
  417.7 4.1 copy.101
  421.8 85.7 %while.32 = (s32[]{:T(128)}, bf16[12,1024,64]{1,2,0:T(8,128)(2,1)}, f32[12,1024]{1,0:T(8,128)}, bf16[12,1024,64]{2,1,0:T(8,128)(2,1)}, bf16[12,1024,64]{2,1,0:T(...) while((s32[]{:T(128)}, bf16[12,1024,64]{1,2,0:T(8,128)(2,1)}, ...), condition=%wide.region_8.9_spmd.clone.clone, body=%wide.region_5.8_spmd.clone.sunk.clone | while | flops 284163072 | bytes 13695065 | solution.py:150
  424.6 3.0 fusion.195
  431.8 3.0 fusion.195
  438.9 3.0 fusion.195
  446.1 3.0 fusion.195
  453.2 3.0 fusion.195
  460.3 3.0 fusion.195
  467.5 3.0 fusion.195
  474.6 3.0 fusion.195
  481.8 3.0 fusion.195
  488.9 3.0 fusion.195
  496.1 3.0 fusion.195
  503.2 3.0 fusion.195
  507.5 21.6 %fusion.64 = f32[4,768,1024]{2,1,0:T(8,128)} fusion(bf16[4,3,768,768]{3,2,1,0:T(8,128)(2,1)} %bitcast.298, bf16[1024,768]{1,0:T(8,128)(2,1)} %param.21), kind=kOutput, calls=%fused_computation.88 | convolution fusion | flops 4831838208 | bytes 18874368 | tf_op jit(solution)/shard_map/td,med->tme/dot_general | solution.py:172
  529.2 12.6 copy.133
  541.7 6.6 copy.105
  548.4 4.0 fusion.140
  555.4 41.0 %convert_reduce_fusion = (f32[3072]{0:T(1024)}, bf16[1024,3072]{1,0:T(8,128)(2,1)}, f32[1024,3072]{1,0:T(8,128)}, f32[1024,3072]{1,0:T(8,128)}) fusion(f32[1024,3072]{1,0:T(8,128)S(1)} %copy-done.15, f32[3072]{0:T(1024)S(1)} %add.234, bf16[3072,768]{1,0:T(8,128)(2,1)} %bitcast.291, f32[1024,768]{0,1:T(8,128)S(1)} %get-tuple-element.370, ...), kind=kOutput, calls=%fused_computation.58 | convolution fusion | flops 5071696896 | bytes 51943424 | tf_op jit(solution)/shard_map/td,mde->tme/dot_general | solution.py:159
  596.4 12.8 multiply_convert_fusion.1
  609.2 8.7 copy.137
  617.9 9.0 convolution_convert_fusion
  629.6 8.8 copy.138
  638.4 9.8 fusion.141
  648.2 3.5 copy.112
  651.8 3.9 multiply_reduce_fusion.1
  659.0 4.4 convolution_convert_fusion.1
  663.4 4.1 copy.113
  667.5 10.4 convert_bitcast_fusion
  678.5 159.2 %while.33 = (s32[]{:T(128)}, f32[12,1024,64]{1,2,0:T(8,128)}, f32[12,1024,64]{1,2,0:T(8,128)}, bf16[12,1024,64]{1,2,0:T(8,128)(2,1)}, bf16[12,1024,64]{2,1,0:T(8...) while((s32[]{:T(128)}, f32[12,1024,64]{1,2,0:T(8,128)}, ...), condition=%wide.region_15.16_spmd.clone.clone, body=%wide.region_13.15_spmd.clone.sunk.clone | while | flops 681704448 | bytes 34112624 | solution.py:214
  681.2 2.6 multiply_reduce_fusion.11
  721.1 2.6 multiply_reduce_fusion.11
  747.5 2.6 multiply_reduce_fusion.11
  774.0 2.6 multiply_reduce_fusion.11
  837.8 12.0 multiply_add_fusion.1
  852.2 7.8 multiply_add_fusion
  872.3 48.2 %reduce-scatter.4.cloned.1.call-done = bf16[1,768,768]{2,1,0:T(8,128)(2,1)} async-done(((bf16[4,768,768]{2,1,0:T(8,128)(2,1)}), bf16[1,768,768]{2,1,0:T(8,128)(2,1)}) %reduce-scatter.4.cloned.1.call-update) | async-done | bytes 1179664 | tf_op jit(solution)/shard_map/reduce_scatter | solution.py:258
  920.5 5.4 maximum_convert_fusion
  931.0 10.8 fusion.75
  944.4 3.3 fusion.114
  947.7 2.8 fusion.115
  950.5 3.2 fusion.133
  956.1 3.3 convert_reduce_fusion.2
  959.3 3.6 copy.125
  967.7 91.3 %psum.15 = f32[14,768]{1,0:T(8,128)S(1)} all-reduce(f32[14,768]{1,0:T(8,128)S(1)} %concatenate.18), channel_id=1, replica_groups=mesh['dp'=8,'mlp'=4] {'dp','mlp'}, use_global_device_ids=true, to_apply=%region_39.40 | all-reduce | flops 10752 | bytes 86016 | tf_op jit(solution)/shard_map/psum | solution.py:253
  1061.1 936.6 %all-gather.7.cloned.1.call-done = f32[24,768,768]{2,1,0:T(8,128)} async-done(((f32[3,768,768]{2,1,0:T(8,128)}), f32[24,768,768]{2,1,0:T(8,128)}) %all-gather.7.cloned.1.call-update) | async-done | bytes 56623120 | tf_op jit(solution)/shard_map/all_gather | solution.py:19
  1997.7 21.5 %reduce_sum.277 = f32[3,768,768]{2,1,0:T(8,128)} reduce(f32[8,3,768,768]{3,2,1,0:T(8,128)} %bitcast.276, f32[]{:T(128)} %constant.45.clone.1), dimensions={0}, to_apply=%region_23.24 | reduce | flops 12386304 | bytes 63700996 | tf_op jit(solution)/shard_map/reduce_sum | solution.py:20
  2019.2 4.5 fusion.90
  2023.7 11.4 fusion.84
  2035.1 9.1 fusion.82
  2044.2 11.5 fusion.79
  2055.7 8.6 multiply_reduce_fusion.4
  2065.1 4.7 fusion.76
  (318 shorter events, 249.8 us)
Async XLA Ops:
  7.2 2048.5 %copy-start = (f32[1,1,768,768]{3,2,1,0:T(8,128)S(1)}, f32[1,1,768,768]{3,2,1,0:T(8,128)}, u32[]{:S(2)}) copy-start(f32[1,1,768,768]{3,2,1,0:T(8,128)} %param.30) | copy-start | bytes 7077892
  7.2 374.6 %all-gather.5.cloned.1.call-start = ((), (), s32[]{:S(2)}) async-start(), calls=%async_computation.6 | async-start | bytes 17694720 | tf_op jit(solution)/shard_map/all_gather | solution.py:106
  292.3 580.0 %reduce-scatter.8.cloned.1.call-start = ((), (), s32[]{:S(2)}) async-start(), calls=%async_computation.5 | async-start | bytes 5898240 | tf_op jit(solution)/shard_map/reduce_scatter | solution.py:264
  292.5 1.1 copy-start.9
  293.7 3.8 copy-start.39
  293.7 4.0 slice-start
  293.7 4.0 copy-start.21
  293.7 4.0 copy-start.54
  293.7 4.0 copy-start.55
  294.8 8.3 copy-start.51
  294.8 8.3 copy-start.52
  297.5 95.9 %copy-start.29 = (f32[12,32]{1,0:T(8,128)}, f32[12,32]{1,0:T(8,128)S(1)}, u32[]{:S(2)}) copy-start(f32[12,32]{1,0:T(8,128)S(1)} %mul.390) | copy-start | bytes 4612
  297.6 95.9 %copy-start.31 = (f32[12,32]{1,0:T(8,128)}, f32[12,32]{1,0:T(8,128)S(1)}, u32[]{:S(2)}) copy-start(f32[12,32]{1,0:T(8,128)S(1)} %mul.385) | copy-start | bytes 4612
  298.4 114.8 %copy-start.41 = (f32[768]{0:T(1024)}, f32[768]{0:T(1024)S(1)}, u32[]{:S(2)}) copy-start(f32[768]{0:T(1024)S(1)} %get-tuple-element.290) | copy-start | bytes 9220
  298.4 114.8 %copy-start.49 = (f32[768]{0:T(1024)}, f32[768]{0:T(1024)S(1)}, u32[]{:S(2)}) copy-start(f32[768]{0:T(1024)S(1)} %get-tuple-element.289) | copy-start | bytes 9220
  300.4 112.9 %copy-start.33 = (f32[1024]{0:T(1024)}, f32[1024]{0:T(1024)S(1)}, u32[]{:S(2)}) copy-start(f32[1024]{0:T(1024)S(1)} %broadcast_multiply_fusion.1) | copy-start | bytes 12292
  302.6 0.6 copy-start.45
  302.6 110.7 %copy-start.43 = (f32[1024]{0:T(1024)}, f32[1024]{0:T(1024)S(1)}, u32[]{:S(2)}) copy-start(f32[1024]{0:T(1024)S(1)} %fusion.118) | copy-start | bytes 12292
  303.2 90.4 %copy-start.35 = (f32[1024]{0:T(1024)}, f32[1024]{0:T(1024)S(1)}, u32[]{:S(2)}) copy-start(f32[1024]{0:T(1024)S(1)} %get-tuple-element.377) | copy-start | bytes 12292
  303.2 90.4 %copy-start.37 = (f32[1024]{0:T(1024)}, f32[1024]{0:T(1024)S(1)}, u32[]{:S(2)}) copy-start(f32[1024]{0:T(1024)S(1)} %get-tuple-element.378) | copy-start | bytes 12292
  381.8 4.9 copy-start.1
  389.7 3.9 copy-start.16
  393.5 7.8 copy-start.18
  548.4 7.0 copy-start.15
  552.4 44.0 %copy-start.4 = (f32[1024,768]{0,1:T(8,128)}, f32[1024,768]{0,1:T(8,128)S(1)}, u32[]{:S(2)}) copy-start(f32[1024,768]{0,1:T(8,128)S(1)} %get-tuple-element.370) | copy-start | bytes 9437188
  626.9 245.4 %reduce-scatter.6.cloned.1.call-start = ((), (), s32[]{:S(2)}) async-start(), calls=%async_computation.4 | async-start | bytes 5898240 | tf_op jit(solution)/shard_map/reduce_scatter | solution.py:261
  651.7 3.9 copy-start.5
  651.7 4.7 copy-start.8
  656.5 1.4 copy-start.13
  657.3 1.7 copy-start.6
  659.0 4.4 copy-start.24
  677.8 0.7 copy-start.22
  677.9 242.6 %reduce-scatter.4.cloned.1.call-start = ((), (), s32[]{:S(2)}) async-start(), calls=%async_computation.3 | async-start | bytes 5898240 | tf_op jit(solution)/shard_map/reduce_scatter | solution.py:258
  678.5 159.2 %copy-start.30 = (f32[12,32]{1,0:T(8,128)S(1)}, f32[12,32]{1,0:T(8,128)}, u32[]{:S(2)}) copy-start(f32[12,32]{1,0:T(8,128)} %copy-done.29) | copy-start | bytes 4612
  678.5 159.2 %copy-start.32 = (f32[12,32]{1,0:T(8,128)S(1)}, f32[12,32]{1,0:T(8,128)}, u32[]{:S(2)}) copy-start(f32[12,32]{1,0:T(8,128)} %copy-done.31) | copy-start | bytes 4612
  678.5 159.2 %copy-start.36 = (f32[1024]{0:T(1024)S(1)}, f32[1024]{0:T(1024)}, u32[]{:S(2)}) copy-start(f32[1024]{0:T(1024)} %copy-done.35) | copy-start | bytes 12292
  678.5 159.2 %copy-start.38 = (f32[1024]{0:T(1024)S(1)}, f32[1024]{0:T(1024)}, u32[]{:S(2)}) copy-start(f32[1024]{0:T(1024)} %copy-done.37) | copy-start | bytes 12292
  837.8 12.2 copy-start.19
  849.7 2.5 copy-start.17
  850.0 17.7 copy-start.26
  860.1 1.4 copy-start.23
  860.1 1.9 copy-start.25
  861.9 4.1 copy-start.27
  861.9 2.0 copy-start.2
  861.9 2.4 copy-start.10
  861.9 2.4 copy-start.34
  861.9 2.4 copy-start.42
  862.0 2.4 copy-start.44
  862.0 2.4 copy-start.50
  871.8 1125.9 %all-gather.7.cloned.1.call-start = ((), (), s32[]{:S(2)}) async-start(), calls=%async_computation.7 | async-start | bytes 63700992 | tf_op jit(solution)/shard_map/all_gather | solution.py:19
  925.9 1.9 copy-start.53
  925.9 5.1 copy-start.48
  944.4 3.3 copy-start.28
  947.7 2.8 copy-start.3
  947.7 2.8 copy-start.11
  950.5 3.2 copy-start.46
  953.7 1.9 copy-start.7
  953.7 2.4 copy-start.14
  959.3 5.5 copy-start.47
  962.9 96.2 %copy-start.40 = (f32[14,768]{1,0:T(8,128)S(1)}, f32[14,768]{1,0:T(8,128)}, u32[]{:S(2)}) copy-start(f32[14,768]{1,0:T(8,128)} %param.22) | copy-start | bytes 129028
  2019.2 4.5 copy-start.56
  2019.2 15.9 copy-start.57
  2023.7 11.4 copy-start.12
  2035.1 9.1 copy-start.20
Sparse Core Ops, SparseCore 0:
  292.4 89.3 all-gather.4
  627.0 47.9 reduce-scatter.7
  678.0 48.3 reduce-scatter.5
  871.9 48.5 reduce-scatter.3
  926.0 1071.6 all-gather.6
